TPU v7x, 32 devices: a whole 2x2x4 slice. The times are simulated.
32 devices in a mesh: case: 2 (over x), axial: 16 (over z, y, core).
Axes of the slice: x: 2, y: 2, z: 4, core: 2. Of those that a mesh axis runs over, the one named last changes fastest.
Arguments:
- forced_pairs: int32 [32, 2], P('case'), parts along dimension 0, may hold values from 0 to 32, as said below
- cell_type: int32 [768, 512], P(('case', 'axial')), parts along dimension 0, may hold values from 0 to 2, as said below
- mean_density: float32 [768, 512], P(('case', 'axial')), parts along dimension 0, may hold values from 0.7 to 1.3
- mean_velocity: float32 [6, 384, 512], P('case', 'axial'), parts along dimension 0, may hold values from -3 to 3
- mean_pressure: float32 [768, 512], P(('case', 'axial')), parts along dimension 0, may hold values from 0.5 to 0.9
- eddy_visc: float32 [768, 512], P(('case', 'axial')), parts along dimension 0, may hold values from 0.02 to 0.3
- forcing: float32 [4, 5, 384, 512], P('case', None, 'axial'), parts along dimension 0, may hold values from -6 to 6
Outputs:
- responses: float32 [32, 2, 5, 384, 512], P('case', None, None, 'axial'), parts along dimension 0
- correction: float32 [4, 384, 512], P('case', 'axial'), parts along dimension 0
There are 2 independent parts, one for each index of `case`. A program takes and returns all parts, laid end to end along the dimension named above; each array names one. Nothing has to cross between parts.
Inputs may be any that keep to these rules, and one draw needn't show every extreme that they name: `forced_pairs`: column 0 is a frequency index of 1 to 32, column 1 an azimuthal wavenumber of 0 to 4. `cell_type`: 0 marks a fluid cell, 1 a sponge cell, 2 a nozzle wall cell.
All inputs are finite; a program needn't handle non-finite values.
Results may differ from a plain program's by a relative error of at most 0.00002.
Values sent between devices are 32-bit elements; how exact they have to be, the bound alone decides.
A program may use at most 128 MiB of HBM per device.

v0:
```python
import functools

import jax
import jax.numpy as jnp
from jax import lax
from jax.experimental import pallas as pl
from jax.experimental.pallas import tpu as pltpu
from jax.sharding import PartitionSpec as P

HEAT_RATIO = 1.4
STEP = 0.1
WAVES = 5
HALO = 8
LANES = 128
F32 = jnp.float32


def exchange_kernel(count, rows, forcing, density, velocity, pressure, visc, cells, halo, halo_cells, send, recv):
    me = lax.axis_index("axial")
    has_low, has_high = me > 0, me < count - 1
    barrier = pltpu.get_barrier_semaphore()

    @pl.when(has_low)
    def _():
        pl.semaphore_signal(barrier, inc=1, device_id={"axial": me - 1}, device_id_type=pl.DeviceIdType.MESH)

    @pl.when(has_high)
    def _():
        pl.semaphore_signal(barrier, inc=1, device_id={"axial": me + 1}, device_id_type=pl.DeviceIdType.MESH)

    @pl.when(has_low & has_high)
    def _():
        pl.semaphore_wait(barrier, 2)

    @pl.when((me == 0) | (me == count - 1))
    def _():
        pl.semaphore_wait(barrier, 1)

    def copies(side):
        start = rows - HALO if side == 0 else 0
        target = me + 1 if side == 0 else me - 1
        cut = pl.ds(start, HALO)
        moves = [
            (forcing.at[:, cut, :], halo.at[side, pl.ds(0, 10)]),
            (velocity.at[:, cut, :], halo.at[side, pl.ds(11, 3)]),
            (density.at[cut, :], halo.at[side, 10]),
            (pressure.at[cut, :], halo.at[side, 14]),
            (visc.at[cut, :], halo.at[side, 15]),
            (cells.at[cut, :], halo_cells.at[side]),
        ]
        return [
            pltpu.make_async_remote_copy(
                src_ref=src,
                dst_ref=dst,
                send_sem=send.at[side, index],
                recv_sem=recv.at[side, index],
                device_id={"axial": target},
                device_id_type=pl.DeviceIdType.MESH,
            )
            for index, (src, dst) in enumerate(moves)
        ]

    up, down = copies(0), copies(1)

    @pl.when(has_high)
    def _():
        for copy in up:
            copy.start()

    @pl.when(has_low)
    def _():
        for copy in down:
            copy.start()

    @pl.when(has_high)
    def _():
        for copy in up:
            copy.wait_send()
        for copy in down:
            copy.wait_recv()

    @pl.when(has_low)
    def _():
        for copy in down:
            copy.wait_send()
        for copy in up:
            copy.wait_recv()


def exchange(count, forcing, density, velocity, pressure, visc, cells):
    rows, radial = density.shape
    return pl.pallas_call(
        functools.partial(exchange_kernel, count, rows),
        out_shape=(
            jax.ShapeDtypeStruct((2, 16, HALO, radial), F32),
            jax.ShapeDtypeStruct((2, HALO, radial), jnp.int32),
        ),
        in_specs=[pl.BlockSpec(memory_space=pl.ANY)] * 6,
        out_specs=(pl.BlockSpec(memory_space=pl.ANY), pl.BlockSpec(memory_space=pl.ANY)),
        scratch_shapes=[pltpu.SemaphoreType.DMA((2, 6)), pltpu.SemaphoreType.DMA((2, 6))],
        compiler_params=pltpu.CompilerParams(collective_id=0, has_side_effects=True),
    )(forcing, density, velocity, pressure, visc, cells)


def response_kernel(
    count, rows, blocks, pairs, forced, forcing, density, velocity, pressure, visc, cells, halo, halo_cells,
    responses, increment, squares,
    field, kind, first, stress, table_p, table_r, result, in_sem, out_sem,
):
    me = lax.axis_index("axial")
    all_rows = rows * count
    ext = rows + 2 * HALO
    own = pl.ds(HALO, rows)

    moves = []
    for block in range(blocks):
        lanes = pl.ds(block * LANES, LANES)
        moves += [
            (forcing.at[:, :, lanes], field.at[pl.ds(0, 10), block + 1, own]),
            (velocity.at[:, :, lanes], field.at[pl.ds(11, 3), block + 1, own]),
            (density.at[:, lanes], field.at[10, block + 1, own]),
            (pressure.at[:, lanes], field.at[14, block + 1, own]),
            (visc.at[:, lanes], field.at[15, block + 1, own]),
            (cells.at[:, lanes], kind.at[block + 1, own]),
        ]
        for side, start in ((0, 0), (1, HALO + rows)):
            edge = pl.ds(start, HALO)
            moves += [
                (halo.at[side, :, :, lanes], field.at[:, block + 1, edge]),
                (halo_cells.at[side, :, lanes], kind.at[block + 1, edge]),
            ]
    copies = [pltpu.make_async_copy(src, dst, in_sem.at[i]) for i, (src, dst) in enumerate(moves)]
    for copy in copies:
        copy.start()
    for side in (0, blocks + 1):
        field[:, side] = jnp.zeros((16, ext, LANES), F32)
        first[:, side] = jnp.zeros((26, ext, LANES), F32)
        stress[:, side] = jnp.zeros((4, ext, LANES), F32)
    for copy in copies:
        copy.wait()

    @pl.when(me == 0)
    def _():
        field[:, :, pl.ds(0, HALO)] = jnp.zeros((16, blocks + 2, HALO, LANES), F32)
        kind[:, pl.ds(0, HALO)] = jnp.zeros((blocks + 2, HALO, LANES), jnp.int32)

    @pl.when(me == count - 1)
    def _():
        field[:, :, pl.ds(HALO + rows, HALO)] = jnp.zeros((16, blocks + 2, HALO, LANES), F32)
        kind[:, pl.ds(HALO + rows, HALO)] = jnp.zeros((blocks + 2, HALO, LANES), jnp.int32)

    lane = lax.broadcasted_iota(jnp.int32, (8, LANES), 1)
    sub = lax.broadcasted_iota(jnp.int32, (8, LANES), 0)
    is_first, is_last = lane == 0, lane == LANES - 1

    def global_row(start):
        return sub + (me * rows + (start - HALO))

    def inside(start):
        row = global_row(start)
        return jnp.where((row >= 0) & (row < all_rows), 1.0, 0.0).astype(F32)

    def inverse_r(c):
        return 1.0 / (((c - 1) * LANES + lane).astype(F32) + 0.5)

    def scale_drive(c, carry):
        for start in range(0, ext, 8):
            envelope = 0.5 + (global_row(start).astype(F32) + 0.5) / all_rows
            for index in range(10):
                field[index, c, pl.ds(start, 8)] = field[index, c, pl.ds(start, 8)] * envelope
        return carry

    lax.fori_loop(1, blocks + 1, scale_drive, 0)

    def at(ref, index, c, start):
        return ref[index, c, pl.ds(start, 8)]

    def axial(ref, index, c, start):
        return [at(ref, index, c, start + offset) for offset in (-2, -1, 1, 2)]

    def radial(ref, index, c, start):
        here = at(ref, index, c, start)
        left = pltpu.roll(jnp.where(is_last, at(ref, index, c - 1, start), here), 1, 1)
        right = pltpu.roll(jnp.where(is_first, at(ref, index, c + 1, start), here), LANES - 1, 1)
        return left, right

    def twelve(near):
        return (near[0] - near[3]) + 8.0 * (near[2] - near[1])

    def coefficients(c, start):
        k = {}
        rho, u, v, w, p = [at(field, 10 + i, c, start) for i in range(5)]
        ir = inverse_r(c)
        nu = STEP * at(field, 15, c, start)
        cell = kind[c, pl.ds(start, 8)]
        damp = jnp.where(cell == 1, 2.0, jnp.where(cell == 2, 10.0, 0.0)).astype(F32)
        inv_rho = STEP / jnp.where(rho > 0.0, rho, 1.0)
        for i in range(5):
            left, right = radial(field, 10 + i, c, start)
            k["x", i] = (-STEP / 12.0) * twelve(axial(field, 10 + i, c, start))
            k["r", i] = (-STEP / 2.0) * (right - left)
        swirl = w * ir
        k["r", 3] = k["r", 3] - STEP * swirl
        k["swirl2"] = (2.0 * STEP) * swirl
        k["u12"] = (-STEP / 12.0) * u
        k["v2"] = (-STEP / 2.0) * v
        k["inviscid"] = 1.0 - STEP * damp
        nu12 = nu * (1.0 / 12.0)
        k["viscous"] = k["inviscid"] - nu * 4.5
        k["m2"] = k["u12"] - nu12
        k["m1"] = 16.0 * nu12 - 8.0 * k["u12"]
        k["p1"] = 16.0 * nu12 + 8.0 * k["u12"]
        k["p2"] = -nu12 - k["u12"]
        slope = 0.5 * nu * ir + k["v2"]
        k["left"] = nu - slope
        k["right"] = nu + slope
        k["rho_div"] = -STEP * rho
        k["p_div"] = (-STEP * HEAT_RATIO) * p
        k["px"] = inv_rho * (-1.0 / 12.0)
        k["pr"] = inv_rho * -0.5
        k["ir"] = ir
        k["turn"] = -STEP * swirl
        k["turn_rho"] = -STEP * rho * ir
        k["turn_w"] = -inv_rho * ir
        k["turn_p"] = k["p_div"] * ir
        k["square"] = -nu * ir * ir
        return k

    def base_operator(k, ref, ids, c, start):
        value, ax, rad = {}, {}, {}
        for i in range(5):
            if ids[i] is not None:
                value[i] = at(ref, ids[i], c, start)
                ax[i] = axial(ref, ids[i], c, start)
                rad[i] = radial(ref, ids[i], c, start)
        div = (1.0 / 12.0) * twelve(ax[1]) + 0.5 * (rad[2][1] - rad[2][0]) + value[2] * k["ir"]
        out = []
        for i in range(5):
            if i in (0, 4):
                term = k["rho_div" if i == 0 else "p_div"] * div
                if i in value:
                    term = term + k["inviscid"] * value[i] + k["u12"] * twelve(ax[i]) + k["v2"] * (rad[i][1] - rad[i][0])
            else:
                term = (
                    k["viscous"] * value[i]
                    + (k["m2"] * ax[i][0] + k["m1"] * ax[i][1])
                    + (k["p1"] * ax[i][2] + k["p2"] * ax[i][3])
                    + (k["left"] * rad[i][0] + k["right"] * rad[i][1])
                )
            if i != 3:
                term = term + k["x", i] * value[1]
            term = term + k["r", i] * value[2]
            if i == 1 and 4 in value:
                term = term + k["px"] * twelve(ax[4])
            if i == 2:
                term = term + k["swirl2"] * value[3]
                if 4 in value:
                    term = term + k["pr"] * (rad[4][1] - rad[4][0])
            out.append(term)
        return out

    def turn_operator(k, q):
        out = [None] * 5
        for i in range(5):
            if q[i] is not None:
                out[i] = k["turn"] * q[i]
        for i, source, name in ((0, 3, "turn_rho"), (3, 4, "turn_w"), (4, 3, "turn_p")):
            if q[source] is not None:
                extra = k[name] * q[source]
                out[i] = extra if out[i] is None else out[i] + extra
        return out

    def base(k, ref, ids, c, start):
        out = base_operator(k, ref, ids, c, start)
        return out

    def first_stage(c, carry):
        for start in range(4, rows + 2 * HALO - 4, 8):
            k = coefficients(c, start)
            keep = inside(start)
            for part in range(2):
                d = [at(field, part * 5 + i, c, start) for i in range(5)]
                moved = base(k, field, [part * 5 + i for i in range(5)], c, start)
                turned = turn_operator(k, d)
                for i in range(5):
                    first[part * 5 + i, c, pl.ds(start, 8)] = keep * (moved[i] + STEP * d[i])
                    first[10 + part * 5 + i, c, pl.ds(start, 8)] = keep * turned[i]
                for i in range(1, 4):
                    first[20 + part * 3 + i - 1, c, pl.ds(start, 8)] = keep * (k["square"] * d[i])
        return carry

    lax.fori_loop(1, blocks + 1, first_stage, 0)

    def tables(c, start):
        k = coefficients(c, start)
        window = pl.ds(start, 8)
        for part in range(2):
            other = 1 - part
            sign = -1.0 if part == 0 else 1.0
            h0 = [part * 5 + i for i in range(5)]
            h0_o = [other * 5 + i for i in range(5)]
            h1 = [10 + part * 5 + i for i in range(5)]
            h1_o = [10 + other * 5 + i for i in range(5)]
            h2 = [None] + [20 + part * 3 + i for i in range(3)] + [None]
            h2_o = [None] + [20 + other * 3 + i for i in range(3)] + [None]

            def values(ids):
                return [None if i is None else at(first, i, c, start) for i in ids]

            d = [at(field, part * 5 + i, c, start) for i in range(5)]
            v0, v0_o, v1, v1_o, v2, v2_o = [values(ids) for ids in (h0, h0_o, h1, h1_o, h2, h2_o)]
            e0 = base(k, first, h0, c, start)
            e1 = base(k, first, h1_o, c, start)
            e2 = base(k, first, h2, c, start)
            t0 = turn_operator(k, v0_o)
            t1 = turn_operator(k, v1)
            t2 = turn_operator(k, v2_o)
            for i in range(5):
                a0 = e0[i] + STEP * d[i]
                a1 = e1[i] + t0[i]
                a2 = e2[i] - t1[i]
                a3 = t2[i]
                a4 = None
                if v2[i] is not None:
                    a2 = a2 + k["square"] * v0[i]
                    a3 = a3 + k["square"] * v1_o[i]
                    a4 = k["square"] * v2[i]
                r0 = 2.0 * v0[i] - STEP * d[i]
                for m in range(WAVES):
                    if m == 0:
                        p_m, r_m = a0, r0
                    else:
                        even = a2 if a4 is None else a2 + float(m * m) * a4
                        odd = a1 + float(m * m) * a3
                        p_m = a0 + float(m * m) * even + (sign * m) * odd
                        r_m = r0 + (sign * 2.0 * m) * v1_o[i]
                        if v2[i] is not None:
                            r_m = r_m + float(2 * m * m) * v2[i]
                    table_p[m, part * 5 + i, window] = p_m
                    table_r[m, part * 5 + i, window] = r_m

    def expand(c, start):
        window = pl.ds(start, 8)
        d = [field[i, c, window] for i in range(10)]

        def one(pair, sums):
            alpha = (STEP * 0.05) * forced[pair, 0].astype(F32)
            m = forced[pair, 1]
            square = alpha * alpha
            q = []
            for i in range(10):
                other = (i + 5) % 10
                turned = alpha * table_r[m, other, window]
                even = table_p[m, i, window] - square * d[i]
                q.append(even - turned if i < 5 else even + turned)
            for i in range(10):
                result[c - 1, pair, i, window] = q[i]
            return (
                sums[0] + (q[1] * q[1] + q[6] * q[6]),
                sums[1] + (q[1] * q[2] + q[6] * q[7]),
                sums[2] + (q[2] * q[2] + q[7] * q[7]),
                sums[3] + (q[3] * q[3] + q[8] * q[8]),
            )

        zero = jnp.zeros((8, LANES), F32)
        sums = lax.fori_loop(0, pairs, one, (zero,) * 4, unroll=2)
        keep = inside(start) * (1.0 / pairs)
        for i in range(4):
            stress[i, c, window] = jnp.where(keep > 0.0, sums[i] * keep, 0.0)

    def out_copy(c):
        lanes = pl.ds(pl.multiple_of((c - 1) * LANES, LANES), LANES)
        return pltpu.make_async_copy(result.at[c - 1, :, :, own], responses.at[:, :, :, lanes], out_sem.at[c - 1])

    def second_stage(c, carry):
        for start in range(6, rows + HALO + 2, 8):
            tables(c, start)
        for start in range(6, rows + HALO + 2, 8):
            expand(c, start)
        out_copy(c).start()
        return carry

    lax.fori_loop(1, blocks + 1, second_stage, 0)

    total = jnp.zeros((8, LANES), F32)
    for c in range(1, blocks + 1):
        ir = inverse_r(c)
        for start in range(HALO, HALO + rows, 8):
            nu = at(field, 15, c, start)

            def laplace(index):
                near = axial(field, index, c, start)
                left, right = radial(field, index, c, start)
                here = at(field, index, c, start)
                second = (16.0 * (near[1] + near[2]) - (near[0] + near[3]) - 30.0 * here) * (1.0 / 12.0)
                return second + (right - 2.0 * here + left)

            def along(index):
                return (1.0 / 12.0) * twelve(axial(stress, index, c, start))

            def across(index):
                left, right = radial(stress, index, c, start)
                return 0.5 * (right - left)

            s1, s2, s3 = [at(stress, i, c, start) for i in (1, 2, 3)]
            first_part = nu * laplace(11) - (along(0) + across(1) + s1 * ir)
            second_part = nu * laplace(12) - (along(1) + across(2) + (s2 - s3) * ir)
            place = (pl.ds(start - HALO, 8), pl.ds((c - 1) * LANES, LANES))
            increment[(0,) + place] = first_part
            increment[(1,) + place] = second_part
            total = total + (first_part * first_part + second_part * second_part)
    squares[...] = total
    for c in range(1, blocks + 1):
        out_copy(c).wait()


def respond(count, forced, forcing, density, velocity, pressure, visc, cells, halo, halo_cells):
    rows, radial = density.shape
    pairs = forced.shape[0]
    blocks = radial // LANES
    ext = rows + 2 * HALO
    anywhere = pl.BlockSpec(memory_space=pl.ANY)
    vmem = pl.BlockSpec(memory_space=pltpu.VMEM)
    return pl.pallas_call(
        functools.partial(response_kernel, count, rows, blocks, pairs),
        out_shape=(
            jax.ShapeDtypeStruct((pairs, 10, rows, radial), F32),
            jax.ShapeDtypeStruct((2, rows, radial), F32),
            jax.ShapeDtypeStruct((8, LANES), F32),
        ),
        in_specs=[pl.BlockSpec(memory_space=pltpu.SMEM)] + [anywhere] * 8,
        out_specs=(anywhere, vmem, vmem),
        scratch_shapes=[
            pltpu.VMEM((16, blocks + 2, ext, LANES), F32),
            pltpu.VMEM((blocks + 2, ext, LANES), jnp.int32),
            pltpu.VMEM((26, blocks + 2, ext, LANES), F32),
            pltpu.VMEM((4, blocks + 2, ext, LANES), F32),
            pltpu.VMEM((WAVES, 10, ext, LANES), F32),
            pltpu.VMEM((WAVES, 10, ext, LANES), F32),
            pltpu.VMEM((blocks, pairs, 10, ext, LANES), F32),
            pltpu.SemaphoreType.DMA((blocks * 10,)),
            pltpu.SemaphoreType.DMA((blocks,)),
        ],
        compiler_params=pltpu.CompilerParams(vmem_limit_bytes=50 * 1024 * 1024),
    )(forced, forcing, density, velocity, pressure, visc, cells, halo, halo_cells)


def total_kernel(count, cells, squares, spread, parts, send, recv):
    me = lax.axis_index("axial")
    barrier = pltpu.get_barrier_semaphore()
    others = [lax.rem(me + hop, count) for hop in range(1, count)]
    for other in others:
        pl.semaphore_signal(barrier, inc=1, device_id={"axial": other}, device_id_type=pl.DeviceIdType.MESH)
    pl.semaphore_wait(barrier, count - 1)
    copies = [
        pltpu.make_async_remote_copy(
            src_ref=squares,
            dst_ref=parts.at[hop],
            send_sem=send.at[hop],
            recv_sem=recv.at[hop],
            device_id={"axial": other},
            device_id_type=pl.DeviceIdType.MESH,
        )
        for hop, other in enumerate(others)
    ]
    for copy in copies:
        copy.start()
    for copy in copies:
        copy.wait()
    total = squares[...]
    for hop in range(count - 1):
        total = total + parts[hop]
    total = jnp.sum(jnp.sum(total, axis=1, keepdims=True), axis=0, keepdims=True)
    spread[...] = jnp.broadcast_to(jnp.sqrt(total / cells + 1e-06), (8, LANES))


def spread_of(count, cells, squares):
    vmem = pl.BlockSpec(memory_space=pltpu.VMEM)
    return pl.pallas_call(
        functools.partial(total_kernel, count, cells),
        out_shape=jax.ShapeDtypeStruct((8, LANES), F32),
        in_specs=[vmem],
        out_specs=vmem,
        scratch_shapes=[
            pltpu.VMEM((count - 1, 8, LANES), F32),
            pltpu.SemaphoreType.DMA((count - 1,)),
            pltpu.SemaphoreType.DMA((count - 1,)),
        ],
        compiler_params=pltpu.CompilerParams(collective_id=1, has_side_effects=True),
    )(squares)


def shards(count, forced, cells, density, velocity, pressure, visc, forcing):
    rows, radial = density.shape
    pairs = forced.shape[0]
    drive = forcing.reshape(10, rows, radial)
    halo, halo_cells = exchange(count, drive, density, velocity, pressure, visc, cells)
    responses, increment, squares = respond(
        count, forced, drive, density, velocity, pressure, visc, cells, halo, halo_cells
    )
    spread = spread_of(count, 2 * rows * count * radial, squares)
    return (responses.reshape(pairs, 2, 5, rows, radial), increment / spread[0, 0])


def solution(mesh):
    placed = (
        P("case", None),
        P(("case", "axial"), None),
        P(("case", "axial"), None),
        P("case", "axial", None),
        P(("case", "axial"), None),
        P(("case", "axial"), None),
        P("case", None, "axial", None),
    )
    return jax.shard_map(
        functools.partial(shards, mesh.shape["axial"]),
        mesh=mesh,
        in_specs=placed,
        out_specs=(P("case", None, None, "axial", None), P("case", "axial", None)),
        check_vma=False,
    )
```

profile of v0, /device:TPU:0, one launch (start us, length us, event | category | flops | bytes accessed | tf_op | source)
XLA Modules:
  0.0 41.2 jit_solution(7383383681026993334)
XLA Ops:
  0.6 0.8 %copy.9.forced = s32[16,2]{1,0:T(8,128)S(1)} copy(s32[16,2]{0,1:T(2,128)} %param.7) | data formatting | bytes 256 | tf_op args[0]
  1.4 4.7 %shard_map.86 = (f32[2,16,8,512]{3,2,1,0:T(8,128)}, s32[2,8,512]{2,1,0:T(8,128)}) custom-call(f32[10,24,512]{2,1,0:T(8,128)} %bitcast.3, f32[24,512]{1,0:T(8,128)} %density.3, f32[3,24,512]{2,1,0:T(8,128)} %velocity.3, f32[24,512]{1,0:T(8,128)} %pressure.3, f32[24,512]{1,0:T(8,128)} %visc.3, s32[24,512]{1,0:T(8,128)} %cells.3), custom_call_target="tpu_custom_call" | custom-call | tf_op jit(solution)/shard_map/pallas_call | solution.py:92
  6.1 0.0 copy-start
  6.1 1.0 %copy-done = f32[2,5,24,512]{3,2,1,0:T(8,128)S(1)} copy-done((f32[2,5,24,512]{3,2,1,0:T(8,128)S(1)}, f32[2,5,24,512]{3,2,1,0:T(8,128)}, u32[]{:S(2)}) %copy-start) | copy-done | bytes 491544
  7.1 0.0 copy-start.1
  7.1 0.9 %copy-done.1 = f32[3,24,512]{2,1,0:T(8,128)S(1)} copy-done((f32[3,24,512]{2,1,0:T(8,128)S(1)}, f32[3,24,512]{2,1,0:T(8,128)}, u32[]{:S(2)}) %copy-start.1) | copy-done | bytes 147480
  8.1 0.0 copy-start.2
  8.1 1.0 %copy-done.2 = f32[2,16,8,512]{3,2,1,0:T(8,128)S(1)} copy-done((f32[2,16,8,512]{3,2,1,0:T(8,128)S(1)}, f32[2,16,8,512]{3,2,1,0:T(8,128)}, u32[]{:S(2)}) %copy-start.2) | copy-done | bytes 524312
  9.1 0.0 copy-start.3
  9.1 0.8 %copy-done.3 = f32[24,512]{1,0:T(8,128)S(1)} copy-done((f32[24,512]{1,0:T(8,128)S(1)}, f32[24,512]{1,0:T(8,128)}, u32[]{:S(2)}) %copy-start.3) | copy-done | bytes 49176
  9.9 0.0 copy-start.4
  9.9 0.8 %copy-done.4 = f32[24,512]{1,0:T(8,128)S(1)} copy-done((f32[24,512]{1,0:T(8,128)S(1)}, f32[24,512]{1,0:T(8,128)}, u32[]{:S(2)}) %copy-start.4) | copy-done | bytes 49176
  10.7 0.0 copy-start.5
  10.7 0.8 %copy-done.5 = f32[24,512]{1,0:T(8,128)S(1)} copy-done((f32[24,512]{1,0:T(8,128)S(1)}, f32[24,512]{1,0:T(8,128)}, u32[]{:S(2)}) %copy-start.5) | copy-done | bytes 49176
  11.5 0.0 copy-start.6
  11.5 0.8 %copy-done.6 = s32[24,512]{1,0:T(8,128)S(1)} copy-done((s32[24,512]{1,0:T(8,128)S(1)}, s32[24,512]{1,0:T(8,128)}, u32[]{:S(2)}) %copy-start.6) | copy-done | bytes 49176
  12.3 0.0 copy-start.7
  12.3 0.8 %copy-done.7 = s32[2,8,512]{2,1,0:T(8,128)S(1)} copy-done((s32[2,8,512]{2,1,0:T(8,128)S(1)}, s32[2,8,512]{2,1,0:T(8,128)}, u32[]{:S(2)}) %copy-start.7) | copy-done | bytes 32792
  13.1 10.5 %shard_map.87 = (f32[16,10,24,512]{3,2,1,0:T(8,128)}, f32[2,24,512]{2,1,0:T(8,128)S(1)}, f32[8,128]{1,0:T(8,128)S(1)}) custom-call(s32[16,2]{1,0:T(8,128)S(1)} %copy.9.forced, f32[10,24,512]{2,1,0:T(8,128)S(1)} %bitcast.4, f32[24,512]{1,0:T(8,128)S(1)} %copy-done.3, f32[3,24,512]{2,1,0:T(8,128)S(1)} %copy-done.1, f32[24,512]{1,0:T(8,128)S(1)} %copy-done.4, ...), custom_call_target="tpu_custom_call" | custom-call | tf_op jit(solution)/shard_map/pallas_call | solution.py:424
  23.5 0.0 copy-start.8
  23.5 0.6 %copy-done.8 = f32[8,128]{1,0:T(8,128)} copy-done((f32[8,128]{1,0:T(8,128)}, f32[8,128]{1,0:T(8,128)S(1)}, u32[]{:S(2)}) %copy-start.8) | copy-done | bytes 4120
  24.1 14.5 %shard_map.88 = f32[8,128]{1,0:T(8,128)} custom-call(f32[8,128]{1,0:T(8,128)} %copy-done.8), custom_call_target="tpu_custom_call" | custom-call | tf_op jit(solution)/shard_map/pallas_call | solution.py:479
  38.6 1.3 %slice.3 = f32[1,1]{1,0:T(1,128)} slice(f32[8,128]{1,0:T(8,128)} %shard_map.88), slice={[0:1], [0:1]} | slice | bytes 8 | tf_op jit(solution)/shard_map/slice | solution.py:502
  39.9 1.3 %broadcast_divide_fusion = f32[2,24,512]{2,1,0:T(8,128)} fusion(f32[2,24,512]{2,1,0:T(8,128)S(1)} %get-tuple-element.10, f32[]{:T(128)} %bitcast.2), kind=kLoop, calls=%fused_computation | loop fusion | flops 24576 | bytes 196612 | tf_op jit(solution)/shard_map/div | solution.py:502
Async XLA Ops:
  6.1 1.0 %copy-start = (f32[2,5,24,512]{3,2,1,0:T(8,128)S(1)}, f32[2,5,24,512]{3,2,1,0:T(8,128)}, u32[]{:S(2)}) copy-start(f32[2,5,24,512]{3,2,1,0:T(8,128)} %param.13) | copy-start | bytes 1474564
  7.1 0.9 %copy-start.1 = (f32[3,24,512]{2,1,0:T(8,128)S(1)}, f32[3,24,512]{2,1,0:T(8,128)}, u32[]{:S(2)}) copy-start(f32[3,24,512]{2,1,0:T(8,128)} %velocity.3) | copy-start | bytes 442372
  8.1 1.0 %copy-start.2 = (f32[2,16,8,512]{3,2,1,0:T(8,128)S(1)}, f32[2,16,8,512]{3,2,1,0:T(8,128)}, u32[]{:S(2)}) copy-start(f32[2,16,8,512]{3,2,1,0:T(8,128)} %get-tuple-element.7.halo) | copy-start | bytes 1572868
  9.1 0.8 %copy-start.3 = (f32[24,512]{1,0:T(8,128)S(1)}, f32[24,512]{1,0:T(8,128)}, u32[]{:S(2)}) copy-start(f32[24,512]{1,0:T(8,128)} %density.3) | copy-start | bytes 147460
  9.9 0.8 %copy-start.4 = (f32[24,512]{1,0:T(8,128)S(1)}, f32[24,512]{1,0:T(8,128)}, u32[]{:S(2)}) copy-start(f32[24,512]{1,0:T(8,128)} %pressure.3) | copy-start | bytes 147460
  10.7 0.8 %copy-start.5 = (f32[24,512]{1,0:T(8,128)S(1)}, f32[24,512]{1,0:T(8,128)}, u32[]{:S(2)}) copy-start(f32[24,512]{1,0:T(8,128)} %visc.3) | copy-start | bytes 147460
  11.5 0.8 %copy-start.6 = (s32[24,512]{1,0:T(8,128)S(1)}, s32[24,512]{1,0:T(8,128)}, u32[]{:S(2)}) copy-start(s32[24,512]{1,0:T(8,128)} %cells.3) | copy-start | bytes 147460
  12.3 0.8 %copy-start.7 = (s32[2,8,512]{2,1,0:T(8,128)S(1)}, s32[2,8,512]{2,1,0:T(8,128)}, u32[]{:S(2)}) copy-start(s32[2,8,512]{2,1,0:T(8,128)} %get-tuple-element.8.halo_cells) | copy-start | bytes 98308
  23.5 0.6 %copy-start.8 = (f32[8,128]{1,0:T(8,128)}, f32[8,128]{1,0:T(8,128)S(1)}, u32[]{:S(2)}) copy-start(f32[8,128]{1,0:T(8,128)S(1)} %get-tuple-element.11.squares) | copy-start | bytes 12292
where the time goes:
time: 41.8 us; the launch traced here: 41.2 us
  Pallas kernels  29.7 us (71%)
  local copies, waits for them, and re-layouts  9.52 us (23%)
  other arithmetic  1.27 us (3%)
  between operations  0.68 us (2%)
    pallas_call x1, Pallas kernels, spread_of(): pl.pallas_call(functools.partial(total_kernel, count, cells), out_shape=j...  14.5 us
    pallas_call x1, Pallas kernels, respond(): pl.pallas_call(functools.partial(response_kernel, count, rows, blocks, pa...  10.5 us
    unnamed x19, local copies, waits for them, and re-layouts  8.27 us
    pallas_call x1, Pallas kernels, exchange(): pl.pallas_call(functools.partial(exchange_kernel, count, rows), out_shape...  4.72 us
    div x1, other arithmetic, shards(): increment / spread[0, 0]  1.27 us
    slice x1, local copies, waits for them, and re-layouts, shards(): spread[0, 0]  1.26 us

commit v1 on v0

--- a/solution.py
+++ b/solution.py
@@ -11,6 +11,8 @@
 STEP = 0.1
 WAVES = 5
 HALO = 8
+WIDE = 6
+NARROW = 4
 LANES = 128
 F32 = jnp.float32
 
@@ -37,16 +39,21 @@
         pl.semaphore_wait(barrier, 1)
 
     def copies(side):
-        start = rows - HALO if side == 0 else 0
         target = me + 1 if side == 0 else me - 1
-        cut = pl.ds(start, HALO)
+
+        def cut(reach):
+            return pl.ds(rows - reach if side == 0 else 0, reach)
+
+        def to(reach):
+            return pl.ds(HALO - reach if side == 0 else 0, reach)
+
         moves = [
-            (forcing.at[:, cut, :], halo.at[side, pl.ds(0, 10)]),
-            (velocity.at[:, cut, :], halo.at[side, pl.ds(11, 3)]),
-            (density.at[cut, :], halo.at[side, 10]),
-            (pressure.at[cut, :], halo.at[side, 14]),
-            (visc.at[cut, :], halo.at[side, 15]),
-            (cells.at[cut, :], halo_cells.at[side]),
+            (forcing.at[:, cut(WIDE), :], halo.at[side, pl.ds(0, 10), to(WIDE)]),
+            (velocity.at[:, cut(WIDE), :], halo.at[side, pl.ds(11, 3), to(WIDE)]),
+            (density.at[cut(WIDE), :], halo.at[side, 10, to(WIDE)]),
+            (pressure.at[cut(WIDE), :], halo.at[side, 14, to(WIDE)]),
+            (visc.at[cut(NARROW), :], halo.at[side, 15, to(NARROW)]),
+            (cells.at[cut(NARROW), :], halo_cells.at[side, to(NARROW)]),
         ]
         return [
             pltpu.make_async_remote_copy(
@@ -104,8 +111,8 @@
 
 def response_kernel(
     count, rows, blocks, pairs, forced, forcing, density, velocity, pressure, visc, cells, halo, halo_cells,
-    responses, increment, squares,
-    field, kind, first, stress, table_p, table_r, result, in_sem, out_sem,
+    responses, increment_out, squares_out,
+    increment, squares, field, kind, first, stress, table_p, table_r, result, in_sem, out_sem, end_sem,
 ):
     me = lax.axis_index("axial")
     all_rows = rows * count
@@ -344,8 +351,8 @@
         d = [field[i, c, window] for i in range(10)]
 
         def one(pair, sums):
-            alpha = (STEP * 0.05) * forced[pair, 0].astype(F32)
-            m = forced[pair, 1]
+            alpha = (STEP * 0.05) * forced[0, pair].astype(F32)
+            m = forced[1, pair]
             square = alpha * alpha
             q = []
             for i in range(10):
@@ -409,28 +416,37 @@
             increment[(0,) + place] = first_part
             increment[(1,) + place] = second_part
             total = total + (first_part * first_part + second_part * second_part)
-    squares[...] = total
+    squares[...] = jnp.sum(total, axis=0, keepdims=True)
+    last = [
+        pltpu.make_async_copy(squares, squares_out, end_sem.at[0]),
+        pltpu.make_async_copy(increment, increment_out, end_sem.at[1]),
+    ]
+    for copy in last:
+        copy.start()
+    for copy in last:
+        copy.wait()
     for c in range(1, blocks + 1):
         out_copy(c).wait()
 
 
 def respond(count, forced, forcing, density, velocity, pressure, visc, cells, halo, halo_cells):
     rows, radial = density.shape
-    pairs = forced.shape[0]
+    pairs = forced.shape[1]
     blocks = radial // LANES
     ext = rows + 2 * HALO
-    anywhere = pl.BlockSpec(memory_space=pl.ANY)
-    vmem = pl.BlockSpec(memory_space=pltpu.VMEM)
+    anywhere = pl.BlockSpec(memory_space=pltpu.HBM)
     return pl.pallas_call(
         functools.partial(response_kernel, count, rows, blocks, pairs),
         out_shape=(
             jax.ShapeDtypeStruct((pairs, 10, rows, radial), F32),
             jax.ShapeDtypeStruct((2, rows, radial), F32),
-            jax.ShapeDtypeStruct((8, LANES), F32),
+            jax.ShapeDtypeStruct((1, LANES), F32),
         ),
         in_specs=[pl.BlockSpec(memory_space=pltpu.SMEM)] + [anywhere] * 8,
-        out_specs=(anywhere, vmem, vmem),
+        out_specs=(anywhere, anywhere, anywhere),
         scratch_shapes=[
+            pltpu.VMEM((2, rows, radial), F32),
+            pltpu.VMEM((1, LANES), F32),
             pltpu.VMEM((16, blocks + 2, ext, LANES), F32),
             pltpu.VMEM((blocks + 2, ext, LANES), jnp.int32),
             pltpu.VMEM((26, blocks + 2, ext, LANES), F32),
@@ -440,17 +456,24 @@
             pltpu.VMEM((blocks, pairs, 10, ext, LANES), F32),
             pltpu.SemaphoreType.DMA((blocks * 10,)),
             pltpu.SemaphoreType.DMA((blocks,)),
+            pltpu.SemaphoreType.DMA((2,)),
         ],
-        compiler_params=pltpu.CompilerParams(vmem_limit_bytes=50 * 1024 * 1024),
+        compiler_params=pltpu.CompilerParams(vmem_limit_bytes=67043328),
     )(forced, forcing, density, velocity, pressure, visc, cells, halo, halo_cells)
 
 
-def total_kernel(count, cells, squares, spread, parts, send, recv):
+def normalize_kernel(count, cells, squares, increment, correction, own, held, parts, send, recv, load):
     me = lax.axis_index("axial")
     barrier = pltpu.get_barrier_semaphore()
     others = [lax.rem(me + hop, count) for hop in range(1, count)]
     for other in others:
         pl.semaphore_signal(barrier, inc=1, device_id={"axial": other}, device_id_type=pl.DeviceIdType.MESH)
+    loads = [
+        pltpu.make_async_copy(squares, own, load.at[0]),
+        pltpu.make_async_copy(increment, held, load.at[1]),
+    ]
+    for copy in loads:
+        copy.start()
     pl.semaphore_wait(barrier, count - 1)
     copies = [
         pltpu.make_async_remote_copy(
@@ -465,29 +488,35 @@
     ]
     for copy in copies:
         copy.start()
+    for copy in loads:
+        copy.wait()
     for copy in copies:
         copy.wait()
-    total = squares[...]
+    total = own[...]
     for hop in range(count - 1):
         total = total + parts[hop]
-    total = jnp.sum(jnp.sum(total, axis=1, keepdims=True), axis=0, keepdims=True)
-    spread[...] = jnp.broadcast_to(jnp.sqrt(total / cells + 1e-06), (8, LANES))
-
-
-def spread_of(count, cells, squares):
-    vmem = pl.BlockSpec(memory_space=pltpu.VMEM)
+    total = jnp.sum(total, axis=1, keepdims=True)
+    inverse = 1.0 / jnp.sqrt(total / cells + 1e-06)
+    correction[...] = held[...] * inverse
+
+
+def normalize(count, cells, squares, increment):
+    anywhere = pl.BlockSpec(memory_space=pltpu.HBM)
     return pl.pallas_call(
-        functools.partial(total_kernel, count, cells),
-        out_shape=jax.ShapeDtypeStruct((8, LANES), F32),
-        in_specs=[vmem],
-        out_specs=vmem,
+        functools.partial(normalize_kernel, count, cells),
+        out_shape=jax.ShapeDtypeStruct(increment.shape, F32),
+        in_specs=[anywhere, anywhere],
+        out_specs=pl.BlockSpec(memory_space=pltpu.VMEM),
         scratch_shapes=[
-            pltpu.VMEM((count - 1, 8, LANES), F32),
+            pltpu.VMEM((1, LANES), F32),
+            pltpu.VMEM(increment.shape, F32),
+            pltpu.VMEM((count - 1, 1, LANES), F32),
             pltpu.SemaphoreType.DMA((count - 1,)),
             pltpu.SemaphoreType.DMA((count - 1,)),
+            pltpu.SemaphoreType.DMA((2,)),
         ],
         compiler_params=pltpu.CompilerParams(collective_id=1, has_side_effects=True),
-    )(squares)
+    )(squares, increment)
 
 
 def shards(count, forced, cells, density, velocity, pressure, visc, forcing):
@@ -496,10 +525,10 @@
     drive = forcing.reshape(10, rows, radial)
     halo, halo_cells = exchange(count, drive, density, velocity, pressure, visc, cells)
     responses, increment, squares = respond(
-        count, forced, drive, density, velocity, pressure, visc, cells, halo, halo_cells
+        count, forced.T, drive, density, velocity, pressure, visc, cells, halo, halo_cells
     )
-    spread = spread_of(count, 2 * rows * count * radial, squares)
-    return (responses.reshape(pairs, 2, 5, rows, radial), increment / spread[0, 0])
+    correction = normalize(count, 2 * rows * count * radial, squares, increment)
+    return (responses.reshape(pairs, 2, 5, rows, radial), correction)
 
 
 def solution(mesh):

time: 41.8 us -> 31.1 us (0.74); the launches traced: 41.2 us -> 30.9 us
  local copies, waits for them, and re-layouts: 9.52 us -> 1.54 us
  other arithmetic: 1.27 us -> 0 us
  Pallas kernels: 29.7 us -> 28.7 us
    unnamed x19 -> x1, local copies, waits for them, and re-layouts: 8.27 us -> 1.54 us
    pallas_call x1, Pallas kernels: 14.5 us -> 12.6 us  [normalize(): pl.pallas_call(functools.partial(normalize_kernel, count, cells), out_sha...]
    div x1 -> x0, other arithmetic: 1.27 us -> none  [shards(): increment / spread[0, 0]]
    slice x1 -> x0, local copies, waits for them, and re-layouts: 1.26 us -> none  [shards(): spread[0, 0]]
    pallas_call x1, Pallas kernels: 10.5 us -> 11.4 us  [respond(): pl.pallas_call(functools.partial(response_kernel, count, rows, blocks, pa...]
where the time goes in v1:
time: 31.1 us; the launch traced here: 30.9 us
  Pallas kernels  28.7 us (92%)
  local copies, waits for them, and re-layouts  1.54 us (5%)
  between operations  0.65 us (2%)
    pallas_call x1, Pallas kernels, normalize(): pl.pallas_call(functools.partial(normalize_kernel, count, cells), out_sha...  12.6 us
    pallas_call x1, Pallas kernels, respond(): pl.pallas_call(functools.partial(response_kernel, count, rows, blocks, pa...  11.4 us
    pallas_call x1, Pallas kernels, exchange(): pl.pallas_call(functools.partial(exchange_kernel, count, rows), out_shape...  4.65 us
    unnamed x1, local copies, waits for them, and re-layouts  1.54 us

profile of v1, /device:TPU:0, one launch (start us, length us, event | category | flops | bytes accessed | tf_op | source)
XLA Modules:
  0.0 30.9 jit_solution(6316138427244675947)
XLA Ops:
  0.6 4.6 %shard_map.86 = (f32[2,16,8,512]{3,2,1,0:T(8,128)}, s32[2,8,512]{2,1,0:T(8,128)}) custom-call(f32[10,24,512]{2,1,0:T(8,128)} %bitcast.3, f32[24,512]{1,0:T(8,128)} %density.3, f32[3,24,512]{2,1,0:T(8,128)} %velocity.3, f32[24,512]{1,0:T(8,128)} %pressure.3, f32[24,512]{1,0:T(8,128)} %visc.3, s32[24,512]{1,0:T(8,128)} %cells.3), custom_call_target="tpu_custom_call" | custom-call | tf_op jit(solution)/shard_map/pallas_call | solution.py:99
  5.3 11.4 %shard_map.87 = (f32[16,10,24,512]{3,2,1,0:T(8,128)}, f32[2,24,512]{2,1,0:T(8,128)}, f32[1,128]{1,0:T(1,128)}) custom-call(s32[2,16]{1,0:T(2,128)} %bitcast.5, f32[10,24,512]{2,1,0:T(8,128)} %bitcast.4, f32[24,512]{1,0:T(8,128)} %density.3, f32[3,24,512]{2,1,0:T(8,128)} %velocity.3, f32[24,512]{1,0:T(8,128)} %pressure.3, f32[24,512]{1,0:T(8,128)} %visc.3, ...), custom_call_target="tpu_custom_call" | custom-call | tf_op jit(solution)/shard_map/pallas_call | solution.py:438
  16.7 12.6 %shard_map.88 = f32[2,24,512]{2,1,0:T(8,128)} custom-call(f32[1,128]{1,0:T(1,128)} %get-tuple-element.10.squares, f32[2,24,512]{2,1,0:T(8,128)} %get-tuple-element.11.increment), custom_call_target="tpu_custom_call" | custom-call | tf_op jit(solution)/shard_map/pallas_call | solution.py:505
  29.4 1.5 %copy.10 = f32[2,24,512]{2,1,0:T(8,128)} copy(f32[2,24,512]{2,1,0:T(8,128)} %shard_map.88) | data formatting | bytes 196608

commit v2 on v1

--- a/solution.py
+++ b/solution.py
@@ -109,10 +109,35 @@
     )(forcing, density, velocity, pressure, visc, cells)
 
 
+def at(ref, index, c, start):
+    return ref[index, c, pl.ds(start, 8)]
+
+
+def axial(ref, index, c, start):
+    return [at(ref, index, c, start + offset) for offset in (-2, -1, 1, 2)]
+
+
+def radial_pair(ref, index, c, start):
+    lane = lax.broadcasted_iota(jnp.int32, (8, LANES), 1)
+    here = at(ref, index, c, start)
+    left = pltpu.roll(jnp.where(lane == LANES - 1, at(ref, index, c - 1, start), here), 1, 1)
+    right = pltpu.roll(jnp.where(lane == 0, at(ref, index, c + 1, start), here), LANES - 1, 1)
+    return left, right
+
+
+def twelve(near):
+    return (near[0] - near[3]) + 8.0 * (near[2] - near[1])
+
+
+def inverse_r(c):
+    lane = lax.broadcasted_iota(jnp.int32, (8, LANES), 1)
+    return 1.0 / (((c - 1) * LANES + lane).astype(F32) + 0.5)
+
+
 def response_kernel(
     count, rows, blocks, pairs, forced, forcing, density, velocity, pressure, visc, cells, halo, halo_cells,
-    responses, increment_out, squares_out,
-    increment, squares, field, kind, first, stress, table_p, table_r, result, in_sem, out_sem, end_sem,
+    responses, stress_out, mean_out,
+    field, kind, first, stress, table_p, table_r, result, in_sem, out_sem, end_sem,
 ):
     me = lax.axis_index("axial")
     all_rows = rows * count
@@ -143,22 +168,22 @@
         field[:, side] = jnp.zeros((16, ext, LANES), F32)
         first[:, side] = jnp.zeros((26, ext, LANES), F32)
         stress[:, side] = jnp.zeros((4, ext, LANES), F32)
-    for copy in copies:
-        copy.wait()
-
-    @pl.when(me == 0)
-    def _():
-        field[:, :, pl.ds(0, HALO)] = jnp.zeros((16, blocks + 2, HALO, LANES), F32)
-        kind[:, pl.ds(0, HALO)] = jnp.zeros((blocks + 2, HALO, LANES), jnp.int32)
-
-    @pl.when(me == count - 1)
-    def _():
-        field[:, :, pl.ds(HALO + rows, HALO)] = jnp.zeros((16, blocks + 2, HALO, LANES), F32)
-        kind[:, pl.ds(HALO + rows, HALO)] = jnp.zeros((blocks + 2, HALO, LANES), jnp.int32)
-
-    lane = lax.broadcasted_iota(jnp.int32, (8, LANES), 1)
+    def settle(block):
+        for copy in copies[10 * block : 10 * block + 10]:
+            copy.wait()
+        c = block + 1
+
+        @pl.when(me == 0)
+        def _():
+            field[:, c, pl.ds(0, HALO)] = jnp.zeros((16, HALO, LANES), F32)
+            kind[c, pl.ds(0, HALO)] = jnp.zeros((HALO, LANES), jnp.int32)
+
+        @pl.when(me == count - 1)
+        def _():
+            field[:, c, pl.ds(HALO + rows, HALO)] = jnp.zeros((16, HALO, LANES), F32)
+            kind[c, pl.ds(HALO + rows, HALO)] = jnp.zeros((HALO, LANES), jnp.int32)
+
     sub = lax.broadcasted_iota(jnp.int32, (8, LANES), 0)
-    is_first, is_last = lane == 0, lane == LANES - 1
 
     def global_row(start):
         return sub + (me * rows + (start - HALO))
@@ -166,9 +191,6 @@
     def inside(start):
         row = global_row(start)
         return jnp.where((row >= 0) & (row < all_rows), 1.0, 0.0).astype(F32)
-
-    def inverse_r(c):
-        return 1.0 / (((c - 1) * LANES + lane).astype(F32) + 0.5)
 
     def scale_drive(c, carry):
         for start in range(0, ext, 8):
@@ -176,23 +198,6 @@
             for index in range(10):
                 field[index, c, pl.ds(start, 8)] = field[index, c, pl.ds(start, 8)] * envelope
         return carry
-
-    lax.fori_loop(1, blocks + 1, scale_drive, 0)
-
-    def at(ref, index, c, start):
-        return ref[index, c, pl.ds(start, 8)]
-
-    def axial(ref, index, c, start):
-        return [at(ref, index, c, start + offset) for offset in (-2, -1, 1, 2)]
-
-    def radial(ref, index, c, start):
-        here = at(ref, index, c, start)
-        left = pltpu.roll(jnp.where(is_last, at(ref, index, c - 1, start), here), 1, 1)
-        right = pltpu.roll(jnp.where(is_first, at(ref, index, c + 1, start), here), LANES - 1, 1)
-        return left, right
-
-    def twelve(near):
-        return (near[0] - near[3]) + 8.0 * (near[2] - near[1])
 
     def coefficients(c, start):
         k = {}
@@ -203,7 +208,7 @@
         damp = jnp.where(cell == 1, 2.0, jnp.where(cell == 2, 10.0, 0.0)).astype(F32)
         inv_rho = STEP / jnp.where(rho > 0.0, rho, 1.0)
         for i in range(5):
-            left, right = radial(field, 10 + i, c, start)
+            left, right = radial_pair(field, 10 + i, c, start)
             k["x", i] = (-STEP / 12.0) * twelve(axial(field, 10 + i, c, start))
             k["r", i] = (-STEP / 2.0) * (right - left)
         swirl = w * ir
@@ -239,7 +244,7 @@
             if ids[i] is not None:
                 value[i] = at(ref, ids[i], c, start)
                 ax[i] = axial(ref, ids[i], c, start)
-                rad[i] = radial(ref, ids[i], c, start)
+                rad[i] = radial_pair(ref, ids[i], c, start)
         div = (1.0 / 12.0) * twelve(ax[1]) + 0.5 * (rad[2][1] - rad[2][0]) + value[2] * k["ir"]
         out = []
         for i in range(5):
@@ -296,7 +301,14 @@
                     first[20 + part * 3 + i - 1, c, pl.ds(start, 8)] = keep * (k["square"] * d[i])
         return carry
 
-    lax.fori_loop(1, blocks + 1, first_stage, 0)
+    for block in range(blocks):
+        settle(block)
+        scale_drive(block + 1, 0)
+        if block > 0:
+            first_stage(block, 0)
+    mean_copy = pltpu.make_async_copy(field.at[pl.ds(11, 5)], mean_out, end_sem.at[0])
+    mean_copy.start()
+    first_stage(blocks, 0)
 
     def tables(c, start):
         k = coefficients(c, start)
@@ -389,42 +401,10 @@
 
     lax.fori_loop(1, blocks + 1, second_stage, 0)
 
-    total = jnp.zeros((8, LANES), F32)
-    for c in range(1, blocks + 1):
-        ir = inverse_r(c)
-        for start in range(HALO, HALO + rows, 8):
-            nu = at(field, 15, c, start)
-
-            def laplace(index):
-                near = axial(field, index, c, start)
-                left, right = radial(field, index, c, start)
-                here = at(field, index, c, start)
-                second = (16.0 * (near[1] + near[2]) - (near[0] + near[3]) - 30.0 * here) * (1.0 / 12.0)
-                return second + (right - 2.0 * here + left)
-
-            def along(index):
-                return (1.0 / 12.0) * twelve(axial(stress, index, c, start))
-
-            def across(index):
-                left, right = radial(stress, index, c, start)
-                return 0.5 * (right - left)
-
-            s1, s2, s3 = [at(stress, i, c, start) for i in (1, 2, 3)]
-            first_part = nu * laplace(11) - (along(0) + across(1) + s1 * ir)
-            second_part = nu * laplace(12) - (along(1) + across(2) + (s2 - s3) * ir)
-            place = (pl.ds(start - HALO, 8), pl.ds((c - 1) * LANES, LANES))
-            increment[(0,) + place] = first_part
-            increment[(1,) + place] = second_part
-            total = total + (first_part * first_part + second_part * second_part)
-    squares[...] = jnp.sum(total, axis=0, keepdims=True)
-    last = [
-        pltpu.make_async_copy(squares, squares_out, end_sem.at[0]),
-        pltpu.make_async_copy(increment, increment_out, end_sem.at[1]),
-    ]
-    for copy in last:
-        copy.start()
-    for copy in last:
-        copy.wait()
+    stress_copy = pltpu.make_async_copy(stress, stress_out, end_sem.at[1])
+    stress_copy.start()
+    mean_copy.wait()
+    stress_copy.wait()
     for c in range(1, blocks + 1):
         out_copy(c).wait()
 
@@ -439,14 +419,12 @@
         functools.partial(response_kernel, count, rows, blocks, pairs),
         out_shape=(
             jax.ShapeDtypeStruct((pairs, 10, rows, radial), F32),
-            jax.ShapeDtypeStruct((2, rows, radial), F32),
-            jax.ShapeDtypeStruct((1, LANES), F32),
+            jax.ShapeDtypeStruct((4, blocks + 2, ext, LANES), F32),
+            jax.ShapeDtypeStruct((5, blocks + 2, ext, LANES), F32),
         ),
         in_specs=[pl.BlockSpec(memory_space=pltpu.SMEM)] + [anywhere] * 8,
         out_specs=(anywhere, anywhere, anywhere),
         scratch_shapes=[
-            pltpu.VMEM((2, rows, radial), F32),
-            pltpu.VMEM((1, LANES), F32),
             pltpu.VMEM((16, blocks + 2, ext, LANES), F32),
             pltpu.VMEM((blocks + 2, ext, LANES), jnp.int32),
             pltpu.VMEM((26, blocks + 2, ext, LANES), F32),
@@ -462,18 +440,54 @@
     )(forced, forcing, density, velocity, pressure, visc, cells, halo, halo_cells)
 
 
-def normalize_kernel(count, cells, squares, increment, correction, own, held, parts, send, recv, load):
+def normalize_kernel(
+    count, rows, blocks, size, stress_in, mean_in, increment_out, inverse,
+    stress, field, increment, squares, parts, send, recv, load,
+):
     me = lax.axis_index("axial")
     barrier = pltpu.get_barrier_semaphore()
     others = [lax.rem(me + hop, count) for hop in range(1, count)]
     for other in others:
         pl.semaphore_signal(barrier, inc=1, device_id={"axial": other}, device_id_type=pl.DeviceIdType.MESH)
     loads = [
-        pltpu.make_async_copy(squares, own, load.at[0]),
-        pltpu.make_async_copy(increment, held, load.at[1]),
+        pltpu.make_async_copy(stress_in, stress, load.at[0]),
+        pltpu.make_async_copy(mean_in, field, load.at[1]),
     ]
     for copy in loads:
         copy.start()
+    for copy in loads:
+        copy.wait()
+
+    def force(c, total):
+        ir = inverse_r(c)
+        for start in range(HALO, HALO + rows, 8):
+            nu = at(field, 4, c, start)
+
+            def laplace(index):
+                near = axial(field, index, c, start)
+                left, right = radial_pair(field, index, c, start)
+                here = at(field, index, c, start)
+                second = (16.0 * (near[1] + near[2]) - (near[0] + near[3]) - 30.0 * here) * (1.0 / 12.0)
+                return second + (right - 2.0 * here + left)
+
+            def along(index):
+                return (1.0 / 12.0) * twelve(axial(stress, index, c, start))
+
+            def across(index):
+                left, right = radial_pair(stress, index, c, start)
+                return 0.5 * (right - left)
+
+            s1, s2, s3 = [at(stress, i, c, start) for i in (1, 2, 3)]
+            first_part = nu * laplace(0) - (along(0) + across(1) + s1 * ir)
+            second_part = nu * laplace(1) - (along(1) + across(2) + (s2 - s3) * ir)
+            place = (pl.ds(start - HALO, 8), pl.ds(pl.multiple_of((c - 1) * LANES, LANES), LANES))
+            increment[(0,) + place] = first_part
+            increment[(1,) + place] = second_part
+            total = total + (first_part * first_part + second_part * second_part)
+        return total
+
+    total = lax.fori_loop(1, blocks + 1, force, jnp.zeros((8, LANES), F32))
+    squares[...] = jnp.sum(total, axis=0, keepdims=True)
     pl.semaphore_wait(barrier, count - 1)
     copies = [
         pltpu.make_async_remote_copy(
@@ -488,35 +502,38 @@
     ]
     for copy in copies:
         copy.start()
-    for copy in loads:
-        copy.wait()
+    keep = pltpu.make_async_copy(increment, increment_out, load.at[2])
+    keep.start()
     for copy in copies:
         copy.wait()
-    total = own[...]
+    total = squares[...]
     for hop in range(count - 1):
         total = total + parts[hop]
     total = jnp.sum(total, axis=1, keepdims=True)
-    inverse = 1.0 / jnp.sqrt(total / cells + 1e-06)
-    correction[...] = held[...] * inverse
-
-
-def normalize(count, cells, squares, increment):
+    inverse[...] = jnp.broadcast_to(1.0 / jnp.sqrt(total / size + 1e-06), inverse.shape)
+    keep.wait()
+
+
+def normalize(count, rows, radial, stress, mean):
     anywhere = pl.BlockSpec(memory_space=pltpu.HBM)
+    increment = (2, rows, radial)
     return pl.pallas_call(
-        functools.partial(normalize_kernel, count, cells),
-        out_shape=jax.ShapeDtypeStruct(increment.shape, F32),
+        functools.partial(normalize_kernel, count, rows, radial // LANES, 2 * rows * count * radial),
+        out_shape=(jax.ShapeDtypeStruct(increment, F32), jax.ShapeDtypeStruct((1, radial), F32)),
         in_specs=[anywhere, anywhere],
-        out_specs=pl.BlockSpec(memory_space=pltpu.VMEM),
+        out_specs=(anywhere, pl.BlockSpec(memory_space=pltpu.VMEM)),
         scratch_shapes=[
+            pltpu.VMEM(stress.shape, F32),
+            pltpu.VMEM(mean.shape, F32),
+            pltpu.VMEM(increment, F32),
             pltpu.VMEM((1, LANES), F32),
-            pltpu.VMEM(increment.shape, F32),
             pltpu.VMEM((count - 1, 1, LANES), F32),
             pltpu.SemaphoreType.DMA((count - 1,)),
             pltpu.SemaphoreType.DMA((count - 1,)),
-            pltpu.SemaphoreType.DMA((2,)),
+            pltpu.SemaphoreType.DMA((3,)),
         ],
         compiler_params=pltpu.CompilerParams(collective_id=1, has_side_effects=True),
-    )(squares, increment)
+    )(stress, mean)
 
 
 def shards(count, forced, cells, density, velocity, pressure, visc, forcing):
@@ -524,11 +541,11 @@
     pairs = forced.shape[0]
     drive = forcing.reshape(10, rows, radial)
     halo, halo_cells = exchange(count, drive, density, velocity, pressure, visc, cells)
-    responses, increment, squares = respond(
+    responses, stress, mean = respond(
         count, forced.T, drive, density, velocity, pressure, visc, cells, halo, halo_cells
     )
-    correction = normalize(count, 2 * rows * count * radial, squares, increment)
-    return (responses.reshape(pairs, 2, 5, rows, radial), correction)
+    increment, inverse = normalize(count, rows, radial, stress, mean)
+    return (responses.reshape(pairs, 2, 5, rows, radial), increment * inverse[None])
 
 
 def solution(mesh):

time: 31.1 us -> 30.9 us (level)
  other arithmetic: 0 us -> 1.55 us
  local copies, waits for them, and re-layouts: 1.54 us -> 0 us
    mul x0 -> x1, other arithmetic: none -> 1.55 us  [shards(): increment * inverse[None]]
    unnamed x1 -> x0, local copies, waits for them, and re-layouts: 1.54 us -> none
where the time goes in v2:
time: 30.9 us; the launch traced here: 30.6 us
  Pallas kernels  28.4 us (92%)
  other arithmetic  1.55 us (5%)
  between operations  0.65 us (2%)
    pallas_call x1, Pallas kernels, normalize(): pl.pallas_call(functools.partial(normalize_kernel, count, rows, radial //...  12.6 us
    pallas_call x1, Pallas kernels, respond(): pl.pallas_call(functools.partial(response_kernel, count, rows, blocks, pa...  11.2 us
    pallas_call x1, Pallas kernels, exchange(): pl.pallas_call(functools.partial(exchange_kernel, count, rows), out_shape...  4.65 us
    mul x1, other arithmetic, shards(): increment * inverse[None]  1.55 us

profile of v2, /device:TPU:0, one launch (start us, length us, event | category | flops | bytes accessed | tf_op | source)
XLA Modules:
  0.0 30.6 jit_solution(16397381699181329548)
XLA Ops:
  0.6 4.6 %shard_map.86 = (f32[2,16,8,512]{3,2,1,0:T(8,128)}, s32[2,8,512]{2,1,0:T(8,128)}) custom-call(f32[10,24,512]{2,1,0:T(8,128)} %bitcast.4, f32[24,512]{1,0:T(8,128)} %density.3, f32[3,24,512]{2,1,0:T(8,128)} %velocity.3, f32[24,512]{1,0:T(8,128)} %pressure.3, f32[24,512]{1,0:T(8,128)} %visc.3, s32[24,512]{1,0:T(8,128)} %cells.3), custom_call_target="tpu_custom_call" | custom-call | tf_op jit(solution)/shard_map/pallas_call | solution.py:99
  5.3 11.2 %shard_map.87 = (f32[16,10,24,512]{3,2,1,0:T(8,128)}, f32[4,6,40,128]{3,2,1,0:T(8,128)}, f32[5,6,40,128]{3,2,1,0:T(8,128)}) custom-call(s32[2,16]{1,0:T(2,128)} %bitcast.7, f32[10,24,512]{2,1,0:T(8,128)} %bitcast.5, f32[24,512]{1,0:T(8,128)} %density.3, f32[3,24,512]{2,1,0:T(8,128)} %velocity.3, f32[24,512]{1,0:T(8,128)} %pressure.3, f32[24,512]{1,0:T(8,128)} %visc.3, ...), custom_call_target="tpu_custom_call" | custom-call | tf_op jit(solution)/shard_map/pallas_call | solution.py:418
  16.4 12.6 %shard_map.88 = (f32[2,24,512]{2,1,0:T(8,128)}, f32[1,512]{1,0:T(1,128)}) custom-call(f32[4,6,40,128]{3,2,1,0:T(8,128)} %get-tuple-element.12.stress_in, f32[5,6,40,128]{3,2,1,0:T(8,128)} %get-tuple-element.13.mean_in), custom_call_target="tpu_custom_call" | custom-call | tf_op jit(solution)/shard_map/pallas_call | solution.py:520
  29.1 1.5 %broadcast_multiply_fusion = f32[2,24,512]{2,1,0:T(8,128)} fusion(f32[2,24,512]{2,1,0:T(8,128)} %get-tuple-element.14, f32[512]{0:T(512)} %bitcast.6), kind=kLoop, calls=%fused_computation | loop fusion | flops 24576 | bytes 198656 | tf_op jit(solution)/shard_map/mul | solution.py:548
